TPU v7x, 32 devices: a whole 2x2x4 slice. The times are simulated.
32 devices in a mesh: dp: 8 (over y, x, core), tensor: 4 (over z).
Axes of the slice: x: 2, y: 2, z: 4, core: 2. Of those that a mesh axis runs over, the one named last changes fastest.
Arguments:
- tokens_in: bfloat16 [4096, 1024], P(('dp', 'tensor')), may hold values from -6 to 6
- attn_gain: float32 [1024], replicated, may hold values from 0.1 to 1.9
- w_query: bfloat16 [1024, 2048], P(None, 'tensor'), may hold values from -0.1875 to 0.1875
- w_key: bfloat16 [1024, 1024], P(None, 'tensor'), may hold values from -0.1875 to 0.1875
- w_value: bfloat16 [1024, 1024], P(None, 'tensor'), may hold values from -0.1875 to 0.1875
- query_gain: float32 [128], replicated, may hold values from 0.5 to 2.5, as said below
- key_gain: float32 [128], replicated, may hold values from 0.5 to 2.5, as said below
- w_output: bfloat16 [2048, 1024], P('tensor'), may hold values from -0.5 to 0.5
- mlp_gain: float32 [1024], replicated, may hold values from 0.1 to 1.9
- w_gate: bfloat16 [1024, 3072], P(None, 'tensor'), may hold values from -0.1875 to 0.1875
- w_up: bfloat16 [1024, 3072], P(None, 'tensor'), may hold values from -0.1875 to 0.1875
- w_down: bfloat16 [3072, 1024], P('tensor'), may hold values from -0.109375 to 0.109375
- out_cotangent: bfloat16 [4096, 1024], P(('dp', 'tensor')), may hold values from -6 to 6
Outputs:
- block_out: bfloat16 [4096, 1024], P(('dp', 'tensor'))
- grad_input: bfloat16 [4096, 1024], P(('dp', 'tensor'))
- grad_attn_gain: float32 [1024], replicated
- grad_w_query: float32 [1024, 2048], P('dp', 'tensor')
- grad_w_key: float32 [1024, 1024], P('dp', 'tensor')
- grad_w_value: float32 [1024, 1024], P('dp', 'tensor')
- grad_query_gain: float32 [128], replicated
- grad_key_gain: float32 [128], replicated
- grad_w_output: float32 [2048, 1024], P('tensor', 'dp')
- grad_mlp_gain: float32 [1024], replicated
- grad_w_gate: float32 [1024, 3072], P('dp', 'tensor')
- grad_w_up: float32 [1024, 3072], P('dp', 'tensor')
- grad_w_down: float32 [3072, 1024], P('tensor', 'dp')
Inputs may be any that keep to these rules, and one draw needn't show every extreme that they name: `query_gain`: positive gains. `key_gain`: positive gains.
All inputs are finite; a program needn't handle non-finite values.
Results may differ from a plain program's by a relative error of at most 0.025.
Values may be sent and summed in bfloat16 or wider, within the bound.
A program may use at most 128 MiB of HBM per device.

v0:
```python
import jax
import jax.numpy as jnp
from jax import lax
from jax.sharding import PartitionSpec as P

SEQ = 512
EPS = 1e-06
THETA = 1000000.0


def rope_tables(length, head_width):
    half_width = head_width // 2
    inverse_freq = THETA ** (-(jnp.arange(half_width, dtype=jnp.float32) * 2.0 / head_width))
    positions = jnp.arange(length, dtype=jnp.float32)
    angles = positions[:, None] * inverse_freq[None, :]
    return (jnp.cos(angles)[:, None, :], jnp.sin(angles)[:, None, :])


def rope_apply(values, cosine_table, sine_table):
    half_width = values.shape[-1] // 2
    first_half = values[..., :half_width]
    second_half = values[..., half_width:]
    return jnp.concatenate(
        [
            first_half * cosine_table - second_half * sine_table,
            second_half * cosine_table + first_half * sine_table,
        ],
        axis=-1,
    )


def rope_back(grad_rows, cosine_table, sine_table):
    half_width = grad_rows.shape[-1] // 2
    first_half = grad_rows[..., :half_width]
    second_half = grad_rows[..., half_width:]
    return jnp.concatenate(
        [
            first_half * cosine_table + second_half * sine_table,
            second_half * cosine_table - first_half * sine_table,
        ],
        axis=-1,
    )


def row_scale(values):
    return lax.rsqrt(jnp.mean(values * values, axis=-1, keepdims=True) + EPS)


def norm_back(grad_out, values, scale_rows, gain_row):
    weighted = grad_out * gain_row
    inner_mean = jnp.mean(weighted * values, axis=-1, keepdims=True)
    return scale_rows * weighted - values * scale_rows**3 * inner_mean


def own_rows(values, start, count):
    return lax.dynamic_slice_in_dim(values, start, count, 0)


def causal_scores(grouped, key_seq, factor):
    length = grouped.shape[0]
    scores = (
        jnp.einsum("qgrd,kgd->grqk", grouped, key_seq, preferred_element_type=jnp.float32) * factor
    )
    rows_at = lax.broadcasted_iota(jnp.int32, (length, length), 0)
    cols_at = lax.broadcasted_iota(jnp.int32, (length, length), 1)
    return jnp.where(cols_at <= rows_at, scores, -jnp.inf)


def attend_forward(inputs):
    query_seq, key_seq, value_seq = inputs
    length, head_count, head_width = query_seq.shape
    kv_count = key_seq.shape[1]
    grouped = query_seq.reshape(length, kv_count, head_count // kv_count, head_width)
    scores = causal_scores(grouped, key_seq, head_width ** (-0.5))
    top_score = jnp.max(scores, axis=-1, keepdims=True)
    log_total = top_score + jnp.log(jnp.sum(jnp.exp(scores - top_score), axis=-1, keepdims=True))
    prob_low = jnp.exp(scores - log_total).astype(jnp.bfloat16)
    mixed_seq = jnp.einsum(
        "grqk,kgd->qgrd", prob_low, value_seq, preferred_element_type=jnp.float32
    )
    return (mixed_seq.astype(jnp.bfloat16).reshape(length, head_count, head_width), log_total)


def attend_backward(inputs):
    query_seq, key_seq, value_seq, mixed_seq, log_total, grad_mixed = inputs
    length, head_count, head_width = query_seq.shape
    kv_count = key_seq.shape[1]
    ratio = head_count // kv_count
    factor = head_width ** (-0.5)
    grouped = query_seq.reshape(length, kv_count, ratio, head_width)
    scores = causal_scores(grouped, key_seq, factor)
    prob_full = jnp.exp(scores - log_total)
    prob_low = prob_full.astype(jnp.bfloat16)
    grad_grouped = grad_mixed.reshape(length, kv_count, ratio, head_width)
    inner_rows = jnp.sum(grad_mixed.astype(jnp.float32) * mixed_seq.astype(jnp.float32), axis=-1)
    inner_rows = jnp.transpose(inner_rows.reshape(length, kv_count, ratio), (1, 2, 0))[..., None]
    grad_probs = jnp.einsum(
        "qgrd,kgd->grqk", grad_grouped, value_seq, preferred_element_type=jnp.float32
    )
    grad_scores = (prob_full * (grad_probs - inner_rows)).astype(jnp.bfloat16)
    grad_query = (
        jnp.einsum("grqk,kgd->qgrd", grad_scores, key_seq, preferred_element_type=jnp.float32)
        * factor
    )
    grad_key = (
        jnp.einsum("grqk,qgrd->kgd", grad_scores, grouped, preferred_element_type=jnp.float32)
        * factor
    )
    grad_value = jnp.einsum(
        "grqk,qgrd->kgd", prob_low, grad_grouped, preferred_element_type=jnp.float32
    )
    return (grad_query.reshape(length, head_count, head_width), grad_key, grad_value)


def on_device(
    tokens_in,
    attn_gain,
    w_query,
    w_key,
    w_value,
    query_gain,
    key_gain,
    w_output,
    mlp_gain,
    w_gate,
    w_up,
    w_down,
    out_cotangent,
):
    row_share = tokens_in.shape[0]
    row_start = lax.axis_index("tensor") * row_share
    head_width = query_gain.shape[0]
    head_count = w_query.shape[1] // head_width
    kv_count = w_key.shape[1] // head_width
    cosine_table, sine_table = rope_tables(SEQ, head_width)
    resid_in = lax.all_gather(tokens_in, "tensor", axis=0, tiled=True).astype(jnp.float32)
    scale_one = row_scale(resid_in)
    normed_one = (resid_in * scale_one * attn_gain).astype(jnp.bfloat16)
    tok_count = normed_one.shape[0]
    seq_count = tok_count // SEQ
    query_lin = jnp.dot(normed_one, w_query, preferred_element_type=jnp.float32).reshape(
        tok_count, head_count, head_width
    )
    key_lin = jnp.dot(normed_one, w_key, preferred_element_type=jnp.float32).reshape(
        tok_count, kv_count, head_width
    )
    value_heads = (
        jnp.dot(normed_one, w_value, preferred_element_type=jnp.float32)
        .astype(jnp.bfloat16)
        .reshape(seq_count, SEQ, kv_count, head_width)
    )
    query_scale = row_scale(query_lin)
    key_scale = row_scale(key_lin)
    query_rot = rope_apply(
        (query_lin * query_scale * query_gain).reshape(seq_count, SEQ, head_count, head_width),
        cosine_table,
        sine_table,
    ).astype(jnp.bfloat16)
    key_rot = rope_apply(
        (key_lin * key_scale * key_gain).reshape(seq_count, SEQ, kv_count, head_width),
        cosine_table,
        sine_table,
    ).astype(jnp.bfloat16)
    mixed_heads, log_totals = lax.map(attend_forward, (query_rot, key_rot, value_heads))
    attn_flat = mixed_heads.reshape(tok_count, head_count * head_width)
    attn_part = jnp.dot(attn_flat, w_output, preferred_element_type=jnp.float32)
    hidden = resid_in + lax.psum(attn_part.astype(jnp.bfloat16), "tensor").astype(jnp.float32)
    scale_two = row_scale(hidden)
    normed_two = (hidden * scale_two * mlp_gain).astype(jnp.bfloat16)
    gate_lin = jnp.dot(normed_two, w_gate, preferred_element_type=jnp.float32)
    up_lin = jnp.dot(normed_two, w_up, preferred_element_type=jnp.float32)
    gate_sig = jax.nn.sigmoid(gate_lin)
    activated = (gate_lin * gate_sig * up_lin).astype(jnp.bfloat16)
    mlp_part = jnp.dot(activated, w_down, preferred_element_type=jnp.float32)
    output_all = hidden + lax.psum(mlp_part.astype(jnp.bfloat16), "tensor").astype(jnp.float32)
    block_out = own_rows(output_all, row_start, row_share).astype(jnp.bfloat16)
    grad_all = lax.all_gather(out_cotangent, "tensor", axis=0, tiled=True)
    grad_down = jnp.dot(activated.T, grad_all, preferred_element_type=jnp.float32)
    grad_act = jnp.dot(grad_all, w_down.T, preferred_element_type=jnp.float32)
    grad_gate = (grad_act * up_lin * gate_sig * (1.0 + gate_lin * (1.0 - gate_sig))).astype(
        jnp.bfloat16
    )
    grad_up = (grad_act * gate_lin * gate_sig).astype(jnp.bfloat16)
    grad_w_gate = jnp.dot(normed_two.T, grad_gate, preferred_element_type=jnp.float32)
    grad_w_up = jnp.dot(normed_two.T, grad_up, preferred_element_type=jnp.float32)
    back_two = jnp.dot(grad_gate, w_gate.T, preferred_element_type=jnp.float32) + jnp.dot(
        grad_up, w_up.T, preferred_element_type=jnp.float32
    )
    grad_norm_two = lax.psum(back_two, "tensor")
    grad_hidden = grad_all.astype(jnp.float32) + norm_back(
        grad_norm_two, hidden, scale_two, mlp_gain
    )
    gain_two = jnp.sum(
        own_rows(grad_norm_two, row_start, row_share)
        * own_rows(hidden * scale_two, row_start, row_share),
        axis=0,
    )
    grad_hidden_low = grad_hidden.astype(jnp.bfloat16)
    grad_w_output = jnp.dot(attn_flat.T, grad_hidden_low, preferred_element_type=jnp.float32)
    grad_mixed = (
        jnp.dot(grad_hidden_low, w_output.T, preferred_element_type=jnp.float32)
        .astype(jnp.bfloat16)
        .reshape(seq_count, SEQ, head_count, head_width)
    )
    grad_query_rot, grad_key_rot, grad_values = lax.map(
        attend_backward, (query_rot, key_rot, value_heads, mixed_heads, log_totals, grad_mixed)
    )
    grad_query_pre = rope_back(grad_query_rot, cosine_table, sine_table).reshape(
        tok_count, head_count, head_width
    )
    grad_key_pre = rope_back(grad_key_rot, cosine_table, sine_table).reshape(
        tok_count, kv_count, head_width
    )
    gain_query = jnp.sum(grad_query_pre * query_lin * query_scale, axis=(0, 1))
    gain_key = jnp.sum(grad_key_pre * key_lin * key_scale, axis=(0, 1))
    grad_query_low = (
        norm_back(grad_query_pre, query_lin, query_scale, query_gain)
        .astype(jnp.bfloat16)
        .reshape(tok_count, head_count * head_width)
    )
    grad_key_low = (
        norm_back(grad_key_pre, key_lin, key_scale, key_gain)
        .astype(jnp.bfloat16)
        .reshape(tok_count, kv_count * head_width)
    )
    grad_value_low = grad_values.astype(jnp.bfloat16).reshape(tok_count, kv_count * head_width)
    grad_w_query = jnp.dot(normed_one.T, grad_query_low, preferred_element_type=jnp.float32)
    grad_w_key = jnp.dot(normed_one.T, grad_key_low, preferred_element_type=jnp.float32)
    grad_w_value = jnp.dot(normed_one.T, grad_value_low, preferred_element_type=jnp.float32)
    back_one = (
        jnp.dot(grad_query_low, w_query.T, preferred_element_type=jnp.float32)
        + jnp.dot(grad_key_low, w_key.T, preferred_element_type=jnp.float32)
        + jnp.dot(grad_value_low, w_value.T, preferred_element_type=jnp.float32)
    )
    grad_norm_one = lax.psum(back_one, "tensor")
    grad_input_all = grad_hidden + norm_back(grad_norm_one, resid_in, scale_one, attn_gain)
    grad_input = own_rows(grad_input_all, row_start, row_share).astype(jnp.bfloat16)
    gain_one = jnp.sum(
        own_rows(grad_norm_one, row_start, row_share)
        * own_rows(resid_in * scale_one, row_start, row_share),
        axis=0,
    )
    gain_one, gain_two, gain_query, gain_key = lax.psum(
        (gain_one, gain_two, gain_query, gain_key), ("dp", "tensor")
    )
    grad_w_query, grad_w_key, grad_w_value, grad_w_output, grad_w_gate, grad_w_up, grad_down = (
        lax.psum_scatter(grad_w_query, "dp", scatter_dimension=0, tiled=True),
        lax.psum_scatter(grad_w_key, "dp", scatter_dimension=0, tiled=True),
        lax.psum_scatter(grad_w_value, "dp", scatter_dimension=0, tiled=True),
        lax.psum_scatter(grad_w_output, "dp", scatter_dimension=1, tiled=True),
        lax.psum_scatter(grad_w_gate, "dp", scatter_dimension=0, tiled=True),
        lax.psum_scatter(grad_w_up, "dp", scatter_dimension=0, tiled=True),
        lax.psum_scatter(grad_down, "dp", scatter_dimension=1, tiled=True),
    )
    return (
        block_out,
        grad_input,
        gain_one,
        grad_w_query,
        grad_w_key,
        grad_w_value,
        gain_query,
        gain_key,
        grad_w_output,
        gain_two,
        grad_w_gate,
        grad_w_up,
        grad_down,
    )


def solution(mesh):
    in_specs = (
        P(("dp", "tensor"), None),
        P(),
        P(None, "tensor"),
        P(None, "tensor"),
        P(None, "tensor"),
        P(),
        P(),
        P("tensor", None),
        P(),
        P(None, "tensor"),
        P(None, "tensor"),
        P("tensor", None),
        P(("dp", "tensor"), None),
    )
    out_specs = (
        P(("dp", "tensor"), None),
        P(("dp", "tensor"), None),
        P(),
        P("dp", "tensor"),
        P("dp", "tensor"),
        P("dp", "tensor"),
        P(),
        P(),
        P("tensor", "dp"),
        P(),
        P("dp", "tensor"),
        P("dp", "tensor"),
        P("tensor", "dp"),
    )
    return jax.shard_map(
        on_device, mesh=mesh, in_specs=in_specs, out_specs=out_specs, check_vma=False
    )
```

profile of v0, /device:TPU:0, one launch (start us, length us, event | category | flops | bytes accessed | tf_op | source)
XLA Modules:
  0.0 707.4 jit_solution(18238567241741866970)
XLA Ops:
  9.3 31.0 %all-gather.3.cloned.1.call-done = bf16[512,1024]{1,0:T(8,128)(2,1)} async-done(((bf16[128,1024]{1,0:T(8,128)(2,1)}), bf16[512,1024]{1,0:T(8,128)(2,1)}) %all-gather.3.cloned.1.call-update) | async-done | bytes 1048592 | tf_op jit(solution)/shard_map/all_gather | solution.py:136
  42.4 2.4 multiply_reduce_fusion.4
  50.2 3.0 multiply_reduce_fusion.7
  67.5 50.4 %all-reduce.6.cloned.1.call-done = bf16[512,1024]{1,0:T(8,128)(2,1)} async-done(((bf16[512,1024]{1,0:T(8,128)(2,1)}), bf16[512,1024]{1,0:T(8,128)(2,1)}) %all-reduce.6.cloned.1.call-update) | async-done | bytes 1048592 | tf_op jit(solution)/shard_map/psum | solution.py:167
  117.9 3.1 convert_multiply_fusion
  123.4 2.1 fusion.44
  125.6 2.1 fusion.45
  127.7 19.1 %all-gather.5.cloned.1.call-done = bf16[512,1024]{1,0:T(8,128)(2,1)} async-done(((bf16[128,1024]{1,0:T(8,128)(2,1)}), bf16[512,1024]{1,0:T(8,128)(2,1)}) %all-gather.5.cloned.1.call-update) | async-done | bytes 1048592 | tf_op jit(solution)/shard_map/all_gather | solution.py:177
  146.8 4.7 multiply_convert_fusion.2
  153.5 2.4 convolution_add_fusion
  160.5 3.2 convolution_convert_fusion
  164.0 77.6 %all-reduce.10.cloned.1.call-done = f32[512,1024]{1,0:T(8,128)} async-done(((f32[512,1024]{1,0:T(8,128)}), f32[512,1024]{1,0:T(8,128)}) %all-reduce.10.cloned.1.call-update) | async-done | bytes 2097168 | tf_op jit(solution)/shard_map/psum | solution.py:189
  241.6 2.5 multiply_reduce_fusion.1
  244.4 2.9 subtract_add_fusion
  249.4 3.7 fusion.1
  257.9 2.1 fusion.47
  264.2 2.5 fusion.6
  272.7 3.8 fusion.49
  276.8 3.8 fusion.50
  281.9 3.8 fusion.51
  285.8 2.3 fusion.41
  288.2 3.6 fusion.26
  297.5 85.0 %all-reduce.12.cloned.1.call-done = f32[512,1024]{1,0:T(8,128)} async-done(((f32[512,1024]{1,0:T(8,128)}), f32[512,1024]{1,0:T(8,128)}) %all-reduce.12.cloned.1.call-update) | async-done | bytes 2097168 | tf_op jit(solution)/shard_map/psum | solution.py:235
  382.4 3.3 multiply_reduce_fusion
  387.1 39.4 %all-reduce = (f32[1024]{0:T(1024)}, f32[128]{0:T(128)}, f32[128]{0:T(128)}, f32[1024]{0:T(1024)}) all-reduce(f32[1024]{0:T(1024)S(1)} %multiply_reduce_fusion.6, f32[128]{0:T(128)S(1)} %get-tuple-element.53, f32[128]{0:T(128)S(1)} %get-tuple-element.51, ...), channel_id=1, replica_groups=mesh['dp'=8,'tensor'=4] {'dp','tensor'}, use_global_device_ids=true, to_apply=%region_16.17 | all-reduce | flops 2304 | bytes 18432 | tf_op jit(solution)/shard_map/psum | solution.py:243
  426.5 2.2 fusion.15
  428.8 32.3 %reduce-scatter.12.cloned.1.call-done = f32[128,256]{1,0:T(8,128)} async-done(((f32[1024,256]{1,0:T(8,128)}), f32[128,256]{1,0:T(8,128)}) %reduce-scatter.12.cloned.1.call-update) | async-done | bytes 131088 | tf_op jit(solution)/shard_map/reduce_scatter | solution.py:249
  461.0 50.0 %reduce-scatter.16.cloned.1.call-done = f32[128,768]{1,0:T(8,128)} async-done(((f32[1024,768]{1,0:T(8,128)}), f32[128,768]{1,0:T(8,128)}) %reduce-scatter.16.cloned.1.call-update) | async-done | bytes 393232 | tf_op jit(solution)/shard_map/reduce_scatter | solution.py:251
  511.1 49.9 %reduce-scatter.18.cloned.1.call-done = f32[128,768]{1,0:T(8,128)} async-done(((f32[1024,768]{1,0:T(8,128)}), f32[128,768]{1,0:T(8,128)}) %reduce-scatter.18.cloned.1.call-update) | async-done | bytes 393232 | tf_op jit(solution)/shard_map/reduce_scatter | solution.py:252
  561.0 50.0 %reduce-scatter.20.cloned.1.call-done = f32[768,128]{1,0:T(8,128)} async-done(((f32[768,1024]{1,0:T(8,128)}), f32[768,128]{1,0:T(8,128)}) %reduce-scatter.20.cloned.1.call-update) | async-done | bytes 393232 | tf_op jit(solution)/shard_map/reduce_scatter | solution.py:253
  611.0 44.8 %reduce-scatter.8.cloned.1.call-done = f32[128,512]{1,0:T(8,128)} async-done(((f32[1024,512]{1,0:T(8,128)}), f32[128,512]{1,0:T(8,128)}) %reduce-scatter.8.cloned.1.call-update) | async-done | bytes 262160 | tf_op jit(solution)/shard_map/reduce_scatter | solution.py:247
  655.9 45.0 %reduce-scatter.14.cloned.1.call-done = f32[512,128]{1,0:T(8,128)} async-done(((f32[512,1024]{1,0:T(8,128)}), f32[512,128]{1,0:T(8,128)}) %reduce-scatter.14.cloned.1.call-update) | async-done | bytes 262160 | tf_op jit(solution)/shard_map/reduce_scatter | solution.py:250
  (207 shorter events, 58.4 us)
Async XLA Ops:
  7.2 139.6 %copy-start = (bf16[768,1024]{1,0:T(8,128)(2,1)S(1)}, bf16[768,1024]{1,0:T(8,128)(2,1)}, u32[]{:S(2)}) copy-start(bf16[768,1024]{1,0:T(8,128)(2,1)} %param.24) | copy-start | bytes 4718596
  7.2 35.2 %copy-start.49 = (f32[1024]{0:T(1024)S(1)}, f32[1024]{0:T(1024)}, u32[]{:S(2)}) copy-start(f32[1024]{0:T(1024)} %param.14) | copy-start | bytes 12292
  7.2 33.1 %all-gather.3.cloned.1.call-start = ((), (), s32[]{:S(2)}) async-start(), calls=%async_computation.7 | async-start | bytes 1310720 | tf_op jit(solution)/shard_map/all_gather | solution.py:136
  7.9 110.0 %all-reduce.6.cloned.1.call-start = ((), (), s32[]{:S(2)}) async-start(), calls=%async_computation.8 | async-start | bytes 2097152 | tf_op jit(solution)/shard_map/psum | solution.py:167
  9.0 33.4 %copy-start.19 = (f32[512,64]{1,0:T(8,128)}, f32[512,64]{1,0:T(8,128)S(1)}, u32[]{:S(2)}) copy-start(f32[512,64]{1,0:T(8,128)S(1)} %get-tuple-element.97) | copy-start | bytes 393220
  9.0 33.4 %copy-start.21 = (f32[512,64]{1,0:T(8,128)}, f32[512,64]{1,0:T(8,128)S(1)}, u32[]{:S(2)}) copy-start(f32[512,64]{1,0:T(8,128)S(1)} %get-tuple-element.98) | copy-start | bytes 393220
  9.2 36.8 %copy-start.34 = (f32[512,64]{0,1:T(8,128)}, f32[512,64]{0,1:T(8,128)S(1)}, u32[]{:S(2)}) copy-start(f32[512,64]{0,1:T(8,128)S(1)} %copy.27) | copy-start | bytes 393220
  42.4 19.0 %copy-start.45 = (f32[512]{0:T(512)}, f32[512]{0:T(512)S(1)}, u32[]{:S(2)}) copy-start(f32[512]{0:T(512)S(1)} %get-tuple-element.94) | copy-start | bytes 6148
  42.4 3.4 copy-start.55
  46.0 4.2 copy-start.2
  55.3 3.9 copy-start.14
  66.5 80.3 %all-gather.5.cloned.1.call-start = ((), (), s32[]{:S(2)}) async-start(), calls=%async_computation.10 | async-start | bytes 1310720 | tf_op jit(solution)/shard_map/all_gather | solution.py:177
  67.3 54.4 %copy-start.43 = (f32[1024]{0:T(1024)S(1)}, f32[1024]{0:T(1024)}, u32[]{:S(2)}) copy-start(f32[1024]{0:T(1024)} %param.21) | copy-start | bytes 12292
  67.3 174.3 %all-reduce.10.cloned.1.call-start = ((), (), s32[]{:S(2)}) async-start(), calls=%async_computation.11 | async-start | bytes 4194304 | tf_op jit(solution)/shard_map/psum | solution.py:189
  117.9 3.7 copy-start.6
  146.8 4.7 copy-start.60
  155.9 139.7 %all-reduce.8.cloned.1.call-start = ((), (), s32[]{:S(2)}) async-start(), calls=%async_computation.9 | async-start | bytes 2097152 | tf_op jit(solution)/shard_map/psum | solution.py:175
  163.7 80.4 %copy-start.7 = (bf16[512,1024]{1,0:T(8,128)(2,1)S(1)}, bf16[512,1024]{1,0:T(8,128)(2,1)}, u32[]{:S(2)}) copy-start(bf16[512,1024]{1,0:T(8,128)(2,1)} %all-reduce.6.cloned.1.call-done) | copy-start | bytes 3145732
  163.7 218.7 %all-reduce.12.cloned.1.call-start = ((), (), s32[]{:S(2)}) async-start(), calls=%async_computation.12 | async-start | bytes 4194304 | tf_op jit(solution)/shard_map/psum | solution.py:235
  241.6 2.8 copy-start.17
  244.4 2.9 copy-start.30
  244.4 2.9 copy-start.38
  249.4 3.7 copy-start.25
  249.4 3.7 copy-start.27
  268.6 160.2 %reduce-scatter.10.cloned.1.call-start = ((), (), s32[]{:S(2)}) async-start(), calls=%async_computation.14 | async-start | bytes 1179648 | tf_op jit(solution)/shard_map/reduce_scatter | solution.py:248
  271.0 190.1 %reduce-scatter.12.cloned.1.call-start = ((), (), s32[]{:S(2)}) async-start(), calls=%async_computation.15 | async-start | bytes 1179648 | tf_op jit(solution)/shard_map/reduce_scatter | solution.py:249
  272.6 238.4 %reduce-scatter.16.cloned.1.call-start = ((), (), s32[]{:S(2)}) async-start(), calls=%async_computation.17 | async-start | bytes 3538944 | tf_op jit(solution)/shard_map/reduce_scatter | solution.py:251
  276.5 284.5 %reduce-scatter.18.cloned.1.call-start = ((), (), s32[]{:S(2)}) async-start(), calls=%async_computation.18 | async-start | bytes 3538944 | tf_op jit(solution)/shard_map/reduce_scatter | solution.py:252
  280.7 330.3 %reduce-scatter.20.cloned.1.call-start = ((), (), s32[]{:S(2)}) async-start(), calls=%async_computation.19 | async-start | bytes 3538944 | tf_op jit(solution)/shard_map/reduce_scatter | solution.py:253
  285.8 370.1 %reduce-scatter.8.cloned.1.call-start = ((), (), s32[]{:S(2)}) async-start(), calls=%async_computation.13 | async-start | bytes 2359296 | tf_op jit(solution)/shard_map/reduce_scatter | solution.py:247
  288.2 412.7 %reduce-scatter.14.cloned.1.call-start = ((), (), s32[]{:S(2)}) async-start(), calls=%async_computation.16 | async-start | bytes 2359296 | tf_op jit(solution)/shard_map/reduce_scatter | solution.py:250
  382.4 318.4 %copy-start.1 = (bf16[768,1024]{1,0:T(8,128)(2,1)S(1)}, bf16[768,1024]{1,0:T(8,128)(2,1)}, u32[]{:S(2)}) copy-start(bf16[768,1024]{1,0:T(8,128)(2,1)} %param.24) | copy-start | bytes 4718596
  (43 other events, 67.5 us)
Sparse Core Ops, SparseCore 0:
  9.6 30.6 all-gather.2
  66.7 51.2 all-reduce.5
  119.5 27.2 all-gather.4
  156.1 85.5 all-reduce.9
  243.8 50.9 all-reduce.7
  297.0 85.3 all-reduce.11
  386.2 34.9 reduce-scatter.9
  425.0 36.0 reduce-scatter.11
  465.0 46.0 reduce-scatter.15
  514.9 46.0 reduce-scatter.17
  564.9 46.0 reduce-scatter.19
  614.7 41.0 reduce-scatter.7
  659.7 41.1 reduce-scatter.13
where the time goes:
time: 709 us; the launch traced here: 707 us
  waiting for transfers between devices  537 us (76%)
  matrix products  60.7 us (9%)
  blocking collectives  39.4 us (6%)
  other arithmetic  33.8 us (5%)
  local copies, waits for them, and re-layouts  20.9 us (3%)
  between operations  14.6 us (2%)
    psum x1, waiting for transfers between devices, on_device(): grad_norm_one = lax.psum(back_one, 'tensor')  85 us
    psum x1, waiting for transfers between devices, on_device(): grad_norm_two = lax.psum(back_two, 'tensor')  77.6 us
    psum x1, waiting for transfers between devices, on_device(): lax.psum(attn_part.astype(jnp.bfloat16), 'tensor').astype(jnp.float32)  50.4 us
    reduce_scatter x1, waiting for transfers between devices, on_device(): lax.psum_scatter(grad_w_gate, 'dp', scatter_dimension=0, tiled=True)  50 us
    reduce_scatter x1, waiting for transfers between devices, on_device(): lax.psum_scatter(grad_down, 'dp', scatter_dimension=1, tiled=True)  50 us
    reduce_scatter x1, waiting for transfers between devices, on_device(): lax.psum_scatter(grad_w_up, 'dp', scatter_dimension=0, tiled=True)  49.9 us
    reduce_scatter x1, waiting for transfers between devices, on_device(): lax.psum_scatter(grad_w_output, 'dp', scatter_dimension=1, tiled=True)  45 us
    reduce_scatter x1, waiting for transfers between devices, on_device(): lax.psum_scatter(grad_w_query, 'dp', scatter_dimension=0, tiled=True)  44.8 us
  transfers between devices with their start and end apart: 13, of which 11 were waited for; matrix products, arithmetic and copies ran while one was open for 10% of the time, Pallas kernels for 0%

commit v1 on v0

--- a/solution.py
+++ b/solution.py
@@ -232,7 +232,7 @@
         + jnp.dot(grad_key_low, w_key.T, preferred_element_type=jnp.float32)
         + jnp.dot(grad_value_low, w_value.T, preferred_element_type=jnp.float32)
     )
-    grad_norm_one = lax.psum(back_one, "tensor")
+    grad_norm_one = jnp.sum(lax.all_gather(back_one, "tensor"), axis=0)
     grad_input_all = grad_hidden + norm_back(grad_norm_one, resid_in, scale_one, attn_gain)
     grad_input = own_rows(grad_input_all, row_start, row_share).astype(jnp.bfloat16)
     gain_one = jnp.sum(

time: 709 us -> 770 us (1.086)
  waiting for transfers between devices: 537 us -> 594 us
    all_gather x0 -> x1, waiting for transfers between devices: none -> 148 us  [on_device(): grad_norm_one = jnp.sum(lax.all_gather(back_one, 'tensor'), axis=0)]
    psum x1 -> x0, waiting for transfers between devices: 85 us -> none  [on_device(): grad_norm_one = lax.psum(back_one, 'tensor')]
where the time goes in v1:
time: 770 us; the launch traced here: 769 us
  waiting for transfers between devices  594 us (77%)
  matrix products  60.6 us (8%)
  other arithmetic  39.7 us (5%)
  blocking collectives  38.6 us (5%)
  local copies, waits for them, and re-layouts  21 us (3%)
  between operations  14.6 us (2%)
    all_gather x1, waiting for transfers between devices, on_device(): grad_norm_one = jnp.sum(lax.all_gather(back_one, 'tensor'), axis=0)  148 us
    psum x1, waiting for transfers between devices, on_device(): grad_norm_two = lax.psum(back_two, 'tensor')  77.6 us
    psum x1, waiting for transfers between devices, on_device(): lax.psum(attn_part.astype(jnp.bfloat16), 'tensor').astype(jnp.float32)  50.4 us
    reduce_scatter x1, waiting for transfers between devices, on_device(): lax.psum_scatter(grad_w_gate, 'dp', scatter_dimension=0, tiled=True)  50 us
    reduce_scatter x1, waiting for transfers between devices, on_device(): lax.psum_scatter(grad_down, 'dp', scatter_dimension=1, tiled=True)  50 us
    reduce_scatter x1, waiting for transfers between devices, on_device(): lax.psum_scatter(grad_w_up, 'dp', scatter_dimension=0, tiled=True)  49.9 us
    reduce_scatter x1, waiting for transfers between devices, on_device(): lax.psum_scatter(grad_w_output, 'dp', scatter_dimension=1, tiled=True)  45 us
    reduce_scatter x1, waiting for transfers between devices, on_device(): lax.psum_scatter(grad_w_query, 'dp', scatter_dimension=0, tiled=True)  44.9 us
  transfers between devices with their start and end apart: 13, of which 11 were waited for; matrix products, arithmetic and copies ran while one was open for 10% of the time, Pallas kernels for 0%

profile of v1, /device:TPU:0, one launch (start us, length us, event | category | flops | bytes accessed | tf_op | source)
XLA Modules:
  0.0 769.3 jit_solution(6335201233380734782)
XLA Ops:
  9.3 31.0 %all-gather.5.cloned.1.call-done = bf16[512,1024]{1,0:T(8,128)(2,1)} async-done(((bf16[128,1024]{1,0:T(8,128)(2,1)}), bf16[512,1024]{1,0:T(8,128)(2,1)}) %all-gather.5.cloned.1.call-update) | async-done | bytes 1048592 | tf_op jit(solution)/shard_map/all_gather | solution.py:136
  42.4 2.4 multiply_reduce_fusion.4
  50.2 3.1 multiply_reduce_fusion.7
  67.6 50.4 %all-reduce.5.cloned.1.call-done = bf16[512,1024]{1,0:T(8,128)(2,1)} async-done(((bf16[512,1024]{1,0:T(8,128)(2,1)}), bf16[512,1024]{1,0:T(8,128)(2,1)}) %all-reduce.5.cloned.1.call-update) | async-done | bytes 1048592 | tf_op jit(solution)/shard_map/psum | solution.py:167
  118.0 3.1 convert_multiply_fusion
  123.5 2.1 fusion.44
  127.8 19.1 %all-gather.7.cloned.1.call-done = bf16[512,1024]{1,0:T(8,128)(2,1)} async-done(((bf16[128,1024]{1,0:T(8,128)(2,1)}), bf16[512,1024]{1,0:T(8,128)(2,1)}) %all-gather.7.cloned.1.call-update) | async-done | bytes 1048592 | tf_op jit(solution)/shard_map/all_gather | solution.py:177
  146.9 4.7 multiply_convert_fusion.2
  153.6 2.4 convolution_add_fusion
  160.5 3.2 convolution_convert_fusion
  164.0 77.6 %all-reduce.9.cloned.1.call-done = f32[512,1024]{1,0:T(8,128)} async-done(((f32[512,1024]{1,0:T(8,128)}), f32[512,1024]{1,0:T(8,128)}) %all-reduce.9.cloned.1.call-update) | async-done | bytes 2097168 | tf_op jit(solution)/shard_map/psum | solution.py:189
  241.7 2.5 multiply_reduce_fusion.1
  244.5 2.8 subtract_add_fusion
  249.5 3.7 fusion.1
  258.0 2.1 fusion.47
  264.3 2.5 fusion.6
  272.7 3.8 fusion.49
  276.8 3.8 fusion.50
  281.9 3.8 fusion.51
  285.8 2.3 fusion.41
  288.1 3.6 fusion.26
  297.4 147.8 %all-gather.9.cloned.1.call-done = f32[2048,1024]{1,0:T(8,128)} async-done(((f32[512,1024]{1,0:T(8,128)}), f32[2048,1024]{1,0:T(8,128)}) %all-gather.9.cloned.1.call-update) | async-done | bytes 8388624 | tf_op jit(solution)/shard_map/all_gather | solution.py:235
  445.2 5.9 reduce_sum.146
  451.0 3.4 multiply_reduce_fusion
  455.8 38.6 %all-reduce = (f32[1024]{0:T(1024)}, f32[128]{0:T(128)}, f32[128]{0:T(128)}, f32[1024]{0:T(1024)}) all-reduce(f32[1024]{0:T(1024)S(1)} %multiply_reduce_fusion.6, f32[128]{0:T(128)S(1)} %get-tuple-element.53, f32[128]{0:T(128)S(1)} %get-tuple-element.51, ...), channel_id=1, replica_groups=mesh['dp'=8,'tensor'=4] {'dp','tensor'}, use_global_device_ids=true, to_apply=%region_16.17 | all-reduce | flops 2304 | bytes 18432 | tf_op jit(solution)/shard_map/psum | solution.py:243
  494.4 2.3 fusion.15
  496.7 26.2 %reduce-scatter.12.cloned.1.call-done = f32[128,256]{1,0:T(8,128)} async-done(((f32[1024,256]{1,0:T(8,128)}), f32[128,256]{1,0:T(8,128)}) %reduce-scatter.12.cloned.1.call-update) | async-done | bytes 131088 | tf_op jit(solution)/shard_map/reduce_scatter | solution.py:249
  522.9 50.0 %reduce-scatter.16.cloned.1.call-done = f32[128,768]{1,0:T(8,128)} async-done(((f32[1024,768]{1,0:T(8,128)}), f32[128,768]{1,0:T(8,128)}) %reduce-scatter.16.cloned.1.call-update) | async-done | bytes 393232 | tf_op jit(solution)/shard_map/reduce_scatter | solution.py:251
  572.9 49.9 %reduce-scatter.18.cloned.1.call-done = f32[128,768]{1,0:T(8,128)} async-done(((f32[1024,768]{1,0:T(8,128)}), f32[128,768]{1,0:T(8,128)}) %reduce-scatter.18.cloned.1.call-update) | async-done | bytes 393232 | tf_op jit(solution)/shard_map/reduce_scatter | solution.py:252
  622.8 50.0 %reduce-scatter.20.cloned.1.call-done = f32[768,128]{1,0:T(8,128)} async-done(((f32[768,1024]{1,0:T(8,128)}), f32[768,128]{1,0:T(8,128)}) %reduce-scatter.20.cloned.1.call-update) | async-done | bytes 393232 | tf_op jit(solution)/shard_map/reduce_scatter | solution.py:253
  672.8 44.9 %reduce-scatter.8.cloned.1.call-done = f32[128,512]{1,0:T(8,128)} async-done(((f32[1024,512]{1,0:T(8,128)}), f32[128,512]{1,0:T(8,128)}) %reduce-scatter.8.cloned.1.call-update) | async-done | bytes 262160 | tf_op jit(solution)/shard_map/reduce_scatter | solution.py:247
  717.7 45.0 %reduce-scatter.14.cloned.1.call-done = f32[512,128]{1,0:T(8,128)} async-done(((f32[512,1024]{1,0:T(8,128)}), f32[512,128]{1,0:T(8,128)}) %reduce-scatter.14.cloned.1.call-update) | async-done | bytes 262160 | tf_op jit(solution)/shard_map/reduce_scatter | solution.py:250
  (208 shorter events, 60.4 us)
Async XLA Ops:
  7.2 139.7 %copy-start = (bf16[768,1024]{1,0:T(8,128)(2,1)S(1)}, bf16[768,1024]{1,0:T(8,128)(2,1)}, u32[]{:S(2)}) copy-start(bf16[768,1024]{1,0:T(8,128)(2,1)} %param.24) | copy-start | bytes 4718596
  7.2 35.2 %copy-start.49 = (f32[1024]{0:T(1024)S(1)}, f32[1024]{0:T(1024)}, u32[]{:S(2)}) copy-start(f32[1024]{0:T(1024)} %param.14) | copy-start | bytes 12292
  7.2 33.1 %all-gather.5.cloned.1.call-start = ((), (), s32[]{:S(2)}) async-start(), calls=%async_computation.7 | async-start | bytes 1310720 | tf_op jit(solution)/shard_map/all_gather | solution.py:136
  7.9 110.1 %all-reduce.5.cloned.1.call-start = ((), (), s32[]{:S(2)}) async-start(), calls=%async_computation.8 | async-start | bytes 2097152 | tf_op jit(solution)/shard_map/psum | solution.py:167
  9.0 33.4 %copy-start.19 = (f32[512,64]{1,0:T(8,128)}, f32[512,64]{1,0:T(8,128)S(1)}, u32[]{:S(2)}) copy-start(f32[512,64]{1,0:T(8,128)S(1)} %get-tuple-element.97) | copy-start | bytes 393220
  9.0 33.4 %copy-start.21 = (f32[512,64]{1,0:T(8,128)}, f32[512,64]{1,0:T(8,128)S(1)}, u32[]{:S(2)}) copy-start(f32[512,64]{1,0:T(8,128)S(1)} %get-tuple-element.98) | copy-start | bytes 393220
  9.2 36.8 %copy-start.34 = (f32[512,64]{0,1:T(8,128)}, f32[512,64]{0,1:T(8,128)S(1)}, u32[]{:S(2)}) copy-start(f32[512,64]{0,1:T(8,128)S(1)} %copy.27) | copy-start | bytes 393220
  42.4 19.1 %copy-start.45 = (f32[512]{0:T(512)}, f32[512]{0:T(512)S(1)}, u32[]{:S(2)}) copy-start(f32[512]{0:T(512)S(1)} %get-tuple-element.94) | copy-start | bytes 6148
  42.4 3.4 copy-start.55
  46.1 4.2 copy-start.2
  55.4 3.9 copy-start.14
  66.6 80.3 %all-gather.7.cloned.1.call-start = ((), (), s32[]{:S(2)}) async-start(), calls=%async_computation.10 | async-start | bytes 1310720 | tf_op jit(solution)/shard_map/all_gather | solution.py:177
  67.3 54.3 %copy-start.43 = (f32[1024]{0:T(1024)S(1)}, f32[1024]{0:T(1024)}, u32[]{:S(2)}) copy-start(f32[1024]{0:T(1024)} %param.21) | copy-start | bytes 12292
  67.4 174.3 %all-reduce.9.cloned.1.call-start = ((), (), s32[]{:S(2)}) async-start(), calls=%async_computation.11 | async-start | bytes 4194304 | tf_op jit(solution)/shard_map/psum | solution.py:189
  118.0 3.7 copy-start.6
  146.9 4.7 copy-start.60
  156.0 139.5 %all-reduce.7.cloned.1.call-start = ((), (), s32[]{:S(2)}) async-start(), calls=%async_computation.9 | async-start | bytes 2097152 | tf_op jit(solution)/shard_map/psum | solution.py:175
  163.8 80.4 %copy-start.7 = (bf16[512,1024]{1,0:T(8,128)(2,1)S(1)}, bf16[512,1024]{1,0:T(8,128)(2,1)}, u32[]{:S(2)}) copy-start(bf16[512,1024]{1,0:T(8,128)(2,1)} %all-reduce.5.cloned.1.call-done) | copy-start | bytes 3145732
  163.8 281.4 %all-gather.9.cloned.1.call-start = ((), (), s32[]{:S(2)}) async-start(), calls=%async_computation.19 | async-start | bytes 10485760 | tf_op jit(solution)/shard_map/all_gather | solution.py:235
  241.7 2.8 copy-start.17
  244.5 2.8 copy-start.30
  244.5 2.8 copy-start.38
  249.5 3.7 copy-start.25
  249.5 3.7 copy-start.27
  268.7 228.0 %reduce-scatter.10.cloned.1.call-start = ((), (), s32[]{:S(2)}) async-start(), calls=%async_computation.13 | async-start | bytes 1179648 | tf_op jit(solution)/shard_map/reduce_scatter | solution.py:248
  271.0 251.9 %reduce-scatter.12.cloned.1.call-start = ((), (), s32[]{:S(2)}) async-start(), calls=%async_computation.14 | async-start | bytes 1179648 | tf_op jit(solution)/shard_map/reduce_scatter | solution.py:249
  272.6 300.3 %reduce-scatter.16.cloned.1.call-start = ((), (), s32[]{:S(2)}) async-start(), calls=%async_computation.16 | async-start | bytes 3538944 | tf_op jit(solution)/shard_map/reduce_scatter | solution.py:251
  276.5 346.3 %reduce-scatter.18.cloned.1.call-start = ((), (), s32[]{:S(2)}) async-start(), calls=%async_computation.17 | async-start | bytes 3538944 | tf_op jit(solution)/shard_map/reduce_scatter | solution.py:252
  280.7 392.1 %reduce-scatter.20.cloned.1.call-start = ((), (), s32[]{:S(2)}) async-start(), calls=%async_computation.18 | async-start | bytes 3538944 | tf_op jit(solution)/shard_map/reduce_scatter | solution.py:253
  285.7 432.0 %reduce-scatter.8.cloned.1.call-start = ((), (), s32[]{:S(2)}) async-start(), calls=%async_computation.12 | async-start | bytes 2359296 | tf_op jit(solution)/shard_map/reduce_scatter | solution.py:247
  288.1 474.6 %reduce-scatter.14.cloned.1.call-start = ((), (), s32[]{:S(2)}) async-start(), calls=%async_computation.15 | async-start | bytes 2359296 | tf_op jit(solution)/shard_map/reduce_scatter | solution.py:250
  451.0 311.7 %copy-start.1 = (bf16[768,1024]{1,0:T(8,128)(2,1)S(1)}, bf16[768,1024]{1,0:T(8,128)(2,1)}, u32[]{:S(2)}) copy-start(bf16[768,1024]{1,0:T(8,128)(2,1)} %param.24) | copy-start | bytes 4718596
  (43 other events, 67.4 us)
Sparse Core Ops, SparseCore 0:
  9.6 30.6 all-gather.4
  66.7 51.2 all-reduce.4
  119.6 27.2 all-gather.6
  156.1 85.4 all-reduce.8
  243.9 50.9 all-reduce.6
  296.3 148.8 all-gather.8
  448.9 34.2 reduce-scatter.9
  486.9 35.8 reduce-scatter.11
  526.8 46.0 reduce-scatter.15
  576.7 46.0 reduce-scatter.17
  626.8 46.0 reduce-scatter.19
  676.5 41.1 reduce-scatter.7
  721.6 41.1 reduce-scatter.13
